TPU v7x, 256 devices: a whole 4x4x8 slice. The times are simulated.
256 devices in a mesh: table: 32 (over z, x), scal: 8 (over y, core).
Axes of the slice: x: 4, y: 4, z: 8, core: 2. Of those that a mesh axis runs over, the one named last changes fastest.
Arguments:
- cell_coords: float32 [4, 524288], P(None, ('table', 'scal')), may hold values from 0 to 1
- flamelet_table: float32 [131072, 1024], P('table', 'scal'), may hold values from -15 to 15
- owner_shard: int32 [524288, 1], P(('table', 'scal')), may hold values from 0 to 31; in each aligned block of 64 rows (0 to 63, 64 to 127, ...) at most 5 rows name the same one
- local_bin: int32 [524288], P(('table', 'scal')), may hold values from 0 to 4095
Outputs:
- filtered_fields: float32 [32, 2048, 256], P(None, ('table', 'scal'))
- x_gradient: float32 [32, 2048, 256], P(None, ('table', 'scal'))
Inputs may be any that keep to these rules, and one draw needn't show every extreme that they name: `owner_shard`: in each aligned block of 64 rows (one group of one device's cells) no shard is named by more than 5 rows, a bound that some block reaches.
All inputs are finite; a program needn't handle non-finite values.
Results may differ from a plain program's by a relative error of at most 0.00012.
Values sent between devices are 32-bit elements; how exact they have to be, the bound alone decides.
A program may use at most 128 MiB of HBM per device.

v0:
```python
import jax
import jax.numpy as jnp
import numpy as np
from jax import lax
from jax.sharding import PartitionSpec as P

SCAL_ALL = 32
K = 32
BX = 8
LG = 8
strength = 0.499


def spline_weights(coords):
    linear = [jnp.stack([1.0 - coords[axis_id], coords[axis_id]]) for axis_id in range(3)]
    frac_last = coords[3]
    square = frac_last * frac_last
    cube = square * frac_last
    remain = 1.0 - frac_last
    cubic = jnp.stack(
        [
            remain * remain * remain / 6.0,
            (3.0 * cube - 6.0 * square + 4.0) / 6.0,
            (-3.0 * cube + 3.0 * square + 3.0 * frac_last + 1.0) / 6.0,
            cube / 6.0,
        ]
    )
    product = (
        linear[0][:, None, None, None, :]
        * linear[1][None, :, None, None, :]
        * linear[2][None, None, :, None, :]
        * cubic[None, None, None, :, :]
    )
    return product.reshape(-1, coords.shape[1])


def thomas_solve(below, middle, above, right_side):
    length = middle.shape[0]
    upper_factor = np.zeros(length)
    solved = np.zeros(right_side.shape)
    for row in range(length):
        if row == 0:
            denom = middle[0]
            solved[0] = right_side[0] / denom
        else:
            denom = middle[row] - below[row] * upper_factor[row - 1]
            solved[row] = (right_side[row] - below[row] * solved[row - 1]) / denom
        upper_factor[row] = above[row] / denom
    for row in range(length - 2, -1, -1):
        solved[row] = solved[row] - upper_factor[row] * solved[row + 1]
    return solved


def filter_table(length):
    positions = np.arange(length)
    offset = positions[None, :] - positions[:, None]
    distance = np.abs(offset)
    interior = (positions >= 3) & (positions <= length - 4)
    coeffs = [
        (11.0 + 10.0 * strength) / 16.0,
        (15.0 + 34.0 * strength) / 64.0,
        (-3.0 + 6.0 * strength) / 32.0,
        (1.0 - 2.0 * strength) / 64.0,
    ]
    band = np.zeros((length, length))
    for reach in range(4):
        band = band + np.where(distance == reach, coeffs[reach], 0.0)
    right_side = np.where(interior[:, None], band, np.where(offset == 0, 1.0, 0.0))
    coupling = np.where(interior, strength, 0.0)
    return thomas_solve(coupling, np.ones(length), coupling, right_side).astype(np.float32)


def derivative_table(length):
    positions = np.arange(length)
    offset = positions[None, :] - positions[:, None]
    distance = np.abs(offset)
    direction = np.sign(offset) * 1.0
    boundary = (positions == 0) | (positions == length - 1)
    second = (positions == 1) | (positions == length - 2)
    interior = ~(boundary | second)
    below_diag = np.where(
        interior, 1.0 / 3.0, np.where(second, 0.25, np.where(positions == length - 1, 2.0, 0.0))
    )
    above_diag = np.where(
        interior, 1.0 / 3.0, np.where(second, 0.25, np.where(positions == 0, 2.0, 0.0))
    )
    inner_rows = direction * (
        np.where(distance == 1, 7.0 / 9.0, 0.0) + np.where(distance == 2, 1.0 / 36.0, 0.0)
    )
    second_rows = direction * np.where(distance == 1, 0.75, 0.0)
    first_row = np.where(
        offset == 0, -2.5, np.where(offset == 1, 2.0, np.where(offset == 2, 0.5, 0.0))
    )
    final_row = np.where(
        offset == 0, 2.5, np.where(offset == -1, -2.0, np.where(offset == -2, -0.5, 0.0))
    )
    right_side = np.where(
        interior[:, None],
        inner_rows,
        np.where(
            second[:, None], second_rows, np.where((positions == 0)[:, None], first_row, final_row)
        ),
    )
    return thomas_solve(below_diag, np.ones(length), above_diag, right_side).astype(np.float32)


def on_device(cell_coords, flamelet_table, owner_shard, local_bin):
    table_count = lax.axis_size("table")
    scal_count = lax.axis_size("scal")
    cell_count = cell_coords.shape[1]
    group_size = cell_count // table_count
    capacity = max(2, 5 * group_size // (2 * table_count))
    slot_count = table_count * table_count * capacity
    group_slots = table_count * capacity
    owners = owner_shard[:, 0].reshape(table_count, group_size)
    matches = (
        owners[:, :, None] == jnp.arange(table_count, dtype=jnp.int32)[None, None, :]
    ).astype(jnp.int32)
    group_rank = jnp.sum((jnp.cumsum(matches, axis=1) - 1) * matches, axis=2)
    local_slot = owners * capacity + group_rank
    slot_ids = jnp.arange(group_slots, dtype=jnp.int32)
    placing = (local_slot[:, :, None] == slot_ids[None, None, :]).astype(jnp.float32)
    payload = jnp.concatenate(
        [local_bin.astype(jnp.float32)[None, :], cell_coords], axis=0
    ).reshape(5, table_count, group_size)
    placed = jnp.einsum("fgc,gcq->fgq", payload, placing, precision=lax.Precision.HIGHEST)
    outgoing = (
        placed.reshape(5, table_count, table_count, capacity)
        .transpose(0, 2, 1, 3)
        .reshape(5, table_count, group_slots)
    )
    received = lax.all_to_all(outgoing, "table", split_axis=1, concat_axis=1, tiled=True).reshape(
        5, slot_count
    )
    shard_piece = lax.all_gather(received, "scal", axis=1, tiled=True)
    weights = spline_weights(shard_piece[1:])
    table_rows = jnp.take(flamelet_table, shard_piece[0].astype(jnp.int32), axis=0)
    table_rows = table_rows.reshape(table_rows.shape[0], -1, K)
    looked = jnp.einsum("nsk,kn->sn", table_rows, weights, precision=lax.Precision.HIGHEST)
    looked = looked.reshape(looked.shape[0], scal_count, slot_count)
    grouped = lax.all_to_all(looked, "scal", split_axis=1, concat_axis=0, tiled=True).reshape(
        SCAL_ALL, table_count, table_count, capacity
    )
    length = BX * table_count
    replies = lax.all_to_all(grouped, "table", split_axis=1, concat_axis=1, tiled=True)
    by_group = replies.transpose(0, 2, 1, 3).reshape(SCAL_ALL, table_count, group_slots)
    values = jnp.einsum("sgq,gcq->sgc", by_group, placing, precision=lax.Precision.HIGHEST).reshape(
        SCAL_ALL, table_count, LG, BX
    )
    pencil = lax.all_to_all(values, "table", split_axis=1, concat_axis=3, tiled=True).reshape(
        SCAL_ALL * LG, length
    )
    filter_op = jnp.asarray(filter_table(length).T)
    derivative_op = jnp.asarray(derivative_table(length).T)
    filtered = jnp.dot(pencil, filter_op, precision=lax.Precision.HIGHEST)
    gradient = jnp.dot(filtered, derivative_op, precision=lax.Precision.HIGHEST)
    return (filtered.reshape(SCAL_ALL, LG, length), gradient.reshape(SCAL_ALL, LG, length))


def solution(mesh):
    return jax.shard_map(
        on_device,
        mesh=mesh,
        in_specs=(
            P(None, ("table", "scal")),
            P("table", "scal"),
            P(("table", "scal"), None),
            P(("table", "scal")),
        ),
        out_specs=(P(None, ("table", "scal"), None), P(None, ("table", "scal"), None)),
        check_vma=False,
    )
```

profile of v0, /device:TPU:8, one launch (start us, length us, event | category | flops | bytes accessed | tf_op | source)
XLA Modules:
  0.0 340.3 jit_solution(11872699540350610518)
XLA Ops:
  0.6 0.5 broadcast.128
  1.2 1.5 reduce.5
  2.8 1.7 select_reduce_fusion
  4.6 0.9 concatenate.9
  5.5 0.7 convert_element_type.26
  6.3 1.0 fusion.3
  7.3 0.2 copy.75
  7.6 0.3 copy.76
  8.0 0.3 copy.77
  8.3 0.2 reshape.131
  8.5 21.4 %all_to_all.40 = f32[32,1,800]{2,1,0:T(1,128)S(1)} all-to-all(f32[32,1,800]{2,1,0:T(1,128)S(1)} %reshape.131), channel_id=1, replica_groups=mesh['table'=32,'scal'=8] {'table'}, dimensions={0} | all-to-all | bytes 204800 | tf_op jit(solution)/shard_map/all_to_all | solution.py:132
  29.9 0.6 broadcast.129
  30.5 1.0 reduce.6
  31.5 0.1 reshape.132
  31.7 0.1 reshape.104
  31.8 14.7 %all_gather.3 = f32[5,40960]{1,0:T(8,128)S(1)} all-gather(f32[5,5120]{1,0:T(8,128)S(1)} %reshape.104), channel_id=1, replica_groups=mesh['table'=32,'scal'=8] {'scal'}, dimensions={1}, use_global_device_ids=true | all-gather | bytes 921600 | tf_op jit(solution)/shard_map/all_gather | solution.py:135
  46.5 0.2 compare_select_fusion
  46.7 2.4 slice_convert_fusion
  49.1 134.9 %gather_fusion = f32[40960,128]{1,0:T(8,128)} fusion(f32[4096,128]{1,0:T(8,128)S(1)} %copy-done, s32[40960]{0:T(1024)S(1)} %broadcast_clamp_fusion), kind=kCustom, calls=%fused_computation | custom fusion | bytes 42106880 | tf_op jit(solution)/shard_map/jit(_take)/gather | solution.py:137
  184.1 21.2 %copy.79 = f32[40960,128]{0,1:T(8,128)} copy(f32[40960,128]{1,0:T(8,128)} %gather_fusion) | data formatting | bytes 41943040 | tf_op jit(solution)/shard_map/jit(_take)/gather | solution.py:137
  205.3 0.3 pad_maximum_fusion.3
  205.6 0.6 pad_maximum_fusion.1
  206.2 0.3 broadcast_multiply_fusion.2
  206.5 0.5 broadcast_multiply_fusion.1
  207.0 0.6 pad_maximum_fusion
  207.6 3.4 %broadcast_multiply_fusion = f32[2,2,2,4,40960]{4,3,2,1,0:T(4,128)} fusion(f32[4,40960]{1,0:T(4,128)S(1)} %pad_maximum_fusion, f32[2,2,2,40960]{3,2,1,0:T(2,128)S(1)} %broadcast_multiply_fusion.1), kind=kLoop, calls=%fused_computation.2 | loop fusion | flops 1310720 | bytes 7208960 | tf_op jit(solution)/shard_map/mul | solution.py:29
  211.0 6.1 %mul.131 = f32[32,40960]{1,0:T(8,128)} reshape(f32[2,2,2,4,40960]{4,3,2,1,0:T(4,128)} %broadcast_multiply_fusion) | data formatting | bytes 10485760 | tf_op jit(solution)/shard_map/mul | solution.py:29
  217.2 10.2 %multiply_reduce_fusion = f32[40960,4]{0,1:T(4,128)S(1)} fusion(f32[40960,4,32]{0,2,1:T(8,128)} %bitcast.56, f32[40960,32]{0,1:T(8,128)} %bitcast.57, pred[40960]{0:T(1024)(128)(4,1)S(1)} %compare_and_fusion), kind=kLoop, calls=%fused_computation.1 | loop fusion | flops 15564800 | bytes 26910720 | tf_op jit(solution)/shard_map/nsk,kn->sn/dot_general | solution.py:139
  227.4 14.6 %all_to_all.41 = f32[4,8,5120]{2,0,1:T(4,128)S(1)} all-to-all(f32[4,8,5120]{2,0,1:T(4,128)S(1)} %bitcast.60), channel_id=1, replica_groups=mesh['table'=32,'scal'=8] {'scal'}, dimensions={1} | all-to-all | bytes 1310720 | tf_op jit(solution)/shard_map/all_to_all | solution.py:141
  242.0 17.7 %reshape.106 = f32[32,32,32,5]{3,2,1,0:T(8,128)} reshape(f32[8,4,1,5120]{3,1,0,2:T(4,128)S(1)} %bitcast.61) | data formatting | bytes 1310720 | tf_op jit(solution)/shard_map/reshape | solution.py:141
  259.7 12.5 %copy.81 = f32[32,32,32,5]{2,0,3,1:T(8,128)} copy(f32[32,32,32,5]{3,2,1,0:T(8,128)} %reshape.106) | data formatting | bytes 1310720 | tf_op jit(solution)/shard_map/reshape | solution.py:141
  272.3 2.7 reshape.133
  275.0 23.3 %all_to_all.42 = f32[32,1,5120]{2,1,0:T(1,128)S(1)} all-to-all(f32[32,1,5120]{2,1,0:T(1,128)S(1)} %reshape.133), channel_id=1, replica_groups=mesh['table'=32,'scal'=8] {'table'}, dimensions={0} | all-to-all | bytes 1310720 | tf_op jit(solution)/shard_map/all_to_all | solution.py:145
  298.3 2.2 reduce.7
  300.5 2.4 reshape.134
  302.9 3.0 copy.82
  305.9 1.5 fusion.2
  307.4 0.4 copy.92
  307.8 0.1 bitcast_bitcast_fusion.1
  307.9 0.5 reshape.135
  308.3 17.0 %all_to_all.43 = f32[32,1,2048]{2,1,0:T(1,128)S(1)} all-to-all(f32[32,1,2048]{2,1,0:T(1,128)S(1)} %reshape.135), channel_id=1, replica_groups=mesh['table'=32,'scal'=8] {'table'}, dimensions={0} | all-to-all | bytes 524288 | tf_op jit(solution)/shard_map/all_to_all | solution.py:150
  325.3 1.3 reduce.8
  326.7 1.3 reshape.136
  328.0 1.4 bitcast_bitcast_fusion
  329.5 4.3 %copy.85 = f32[32,1,8,32,8]{4,3,2,0,1:T(8,128)} copy(f32[32,1,8,32,8]{0,4,2,3,1:T(8,128)S(1)} %bitcast_bitcast_fusion) | data formatting | bytes 524288 | tf_op jit(solution)/shard_map/all_to_all | solution.py:150
  333.8 4.0 %reshape.109 = f32[256,256]{1,0:T(8,128)S(1)} reshape(f32[32,1,8,32,8]{4,3,2,0,1:T(8,128)} %copy.85) | data formatting | bytes 524288 | tf_op jit(solution)/shard_map/reshape | solution.py:150
  337.8 1.3 fusion.14
  339.2 1.1 convolution_bitcast_fusion
  (27 shorter events, 0.7 us)
Async XLA Ops:
  0.6 48.5 %copy-start = (f32[4096,128]{1,0:T(8,128)S(1)}, f32[4096,128]{1,0:T(8,128)}, u32[]{:S(2)}) copy-start(f32[4096,128]{1,0:T(8,128)} %param.7) | copy-start | bytes 6291460
  184.1 21.2 %copy-start.4 = (f32[1,40960]{1,0:T(1,128)S(1)}, f32[1,40960]{1,0:T(1,128)}, u32[]{:S(2)}) copy-start(f32[1,40960]{1,0:T(1,128)} %get-tuple-element.5) | copy-start | bytes 491524
  184.1 21.2 %copy-start.5 = (f32[1,40960]{1,0:T(1,128)S(1)}, f32[1,40960]{1,0:T(1,128)}, u32[]{:S(2)}) copy-start(f32[1,40960]{1,0:T(1,128)} %get-tuple-element.10) | copy-start | bytes 491524
  184.1 21.5 %copy-start.3 = (f32[1,40960]{1,0:T(1,128)S(1)}, f32[1,40960]{1,0:T(1,128)}, u32[]{:S(2)}) copy-start(f32[1,40960]{1,0:T(1,128)} %get-tuple-element.12) | copy-start | bytes 491524
  211.0 6.1 %copy-start.6 = (s32[1,40960]{1,0:T(1,128)S(1)}, s32[1,40960]{1,0:T(1,128)}, u32[]{:S(2)}) copy-start(s32[1,40960]{1,0:T(1,128)} %get-tuple-element.2) | copy-start | bytes 491524
  328.0 12.3 %copy-start.1 = (f32[4096,128]{1,0:T(8,128)S(1)}, f32[4096,128]{1,0:T(8,128)}, u32[]{:S(2)}) copy-start(f32[4096,128]{1,0:T(8,128)} %param.7) | copy-start | bytes 6291460
  329.4 9.7 %copy-start.7 = (f32[256,256]{1,0:T(8,128)S(1)}, f32[256,256]{1,0:T(8,128)}, u32[]{:S(2)}) copy-start(f32[256,256]{1,0:T(8,128)} %constant.46.clone) | copy-start | bytes 786436
  339.2 1.1 copy-start.2
where the time goes:
time: 341 us; the launch traced here: 340 us
  local copies, waits for them, and re-layouts  216 us (63%)
  blocking collectives  91.1 us (27%)
  other arithmetic  27 us (8%)
  matrix products  4.91 us (1%)
    gather x2, local copies, waits for them, and re-layouts, on_device(): jnp.take(flamelet_table, shard_piece[0].astype(jnp.int32), axis=0)  156 us
    reshape x2, local copies, waits for them, and re-layouts, on_device(): lax.all_to_all(looked, 'scal', split_axis=1, concat_axis=0, tiled=True)  30.2 us
    all_to_all x1, blocking collectives, on_device(): lax.all_to_all(grouped, 'table', split_axis=1, concat_axis=1, tiled=True)  23.3 us
    all_to_all x1, blocking collectives, on_device(): lax.all_to_all(outgoing, 'table', split_axis=1, concat_axis=1, tiled=True)  21.4 us
    all_to_all x1, blocking collectives, on_device(): lax.all_to_all(values, 'table', split_axis=1, concat_axis=3, tiled=True)  17 us
    all_gather x1, blocking collectives, on_device(): shard_piece = lax.all_gather(received, 'scal', axis=1, tiled=True)  14.7 us
    all_to_all x1, blocking collectives, on_device(): lax.all_to_all(looked, 'scal', split_axis=1, concat_axis=0, tiled=True)  14.6 us
    dot_general x1, other arithmetic, on_device(): jnp.einsum('nsk,kn->sn', table_rows, weights, precision=lax.Precision.HIG...  10.2 us

commit v1 on v0

--- a/solution.py
+++ b/solution.py
@@ -1,3 +1,4 @@
+import functools
 import jax
 import jax.numpy as jnp
 import numpy as np
@@ -9,6 +10,17 @@
 BX = 8
 LG = 8
 strength = 0.499
+
+
+def mix_series(vec, along_axis):
+    taken_in = jax.lax.axis_size(along_axis)
+    main = jnp.split(vec, taken_in, axis=1)
+    last = jnp.stack(main)
+    y2 = jax.lax.all_to_all(last, axis_name=along_axis, split_axis=0, concat_axis=0)
+    return jnp.concatenate(y2, axis=0)
+
+
+ways_measure = functools.partial(mix_series, along_axis="scal")
 
 
 def spline_weights(coords):
@@ -138,9 +150,7 @@
     table_rows = table_rows.reshape(table_rows.shape[0], -1, K)
     looked = jnp.einsum("nsk,kn->sn", table_rows, weights, precision=lax.Precision.HIGHEST)
     looked = looked.reshape(looked.shape[0], scal_count, slot_count)
-    grouped = lax.all_to_all(looked, "scal", split_axis=1, concat_axis=0, tiled=True).reshape(
-        SCAL_ALL, table_count, table_count, capacity
-    )
+    grouped = ways_measure(looked).reshape(SCAL_ALL, table_count, table_count, capacity)
     length = BX * table_count
     replies = lax.all_to_all(grouped, "table", split_axis=1, concat_axis=1, tiled=True)
     by_group = replies.transpose(0, 2, 1, 3).reshape(SCAL_ALL, table_count, group_slots)

time: 341 us -> 344 us (level)
    another operation x0 -> x3, local copies, waits for them, and re-layouts: none -> 30.3 us  [the longest x2 30.2 us: on_device(): ways_measure(looked).reshape(SCAL_ALL, table_count, table_count, capacity)]
    reshape x2 -> x0, local copies, waits for them, and re-layouts: 30.2 us -> none  [on_device(): lax.all_to_all(looked, 'scal', split_axis=1, concat_axis=0, tiled=True)]
    unnamed x24 -> x32, local copies, waits for them, and re-layouts: 7.82 us -> 8.73 us
where the time goes in v1:
time: 344 us; the launch traced here: 343 us
  local copies, waits for them, and re-layouts  217 us (63%)
  blocking collectives  91.1 us (26%)
  other arithmetic  28.8 us (8%)
  matrix products  4.91 us (1%)
    gather x2, local copies, waits for them, and re-layouts, on_device(): jnp.take(flamelet_table, shard_piece[0].astype(jnp.int32), axis=0)  156 us
    another operation x2, local copies, waits for them, and re-layouts, on_device(): ways_measure(looked).reshape(SCAL_ALL, table_count, table_count, capacity)  30.2 us
    all_to_all x1, blocking collectives, on_device(): lax.all_to_all(grouped, 'table', split_axis=1, concat_axis=1, tiled=True)  23.3 us
    all_to_all x1, blocking collectives, on_device(): lax.all_to_all(outgoing, 'table', split_axis=1, concat_axis=1, tiled=True)  21.4 us
    all_to_all x1, blocking collectives, on_device(): lax.all_to_all(values, 'table', split_axis=1, concat_axis=3, tiled=True)  17 us
    all_gather x1, blocking collectives, on_device(): shard_piece = lax.all_gather(received, 'scal', axis=1, tiled=True)  14.7 us
    all_to_all x1, blocking collectives, mix_series(): jax.lax.all_to_all(last, axis_name=along_axis, split_axis=0, concat_axis=0)  14.6 us
    dot_general x1, other arithmetic, on_device(): jnp.einsum('nsk,kn->sn', table_rows, weights, precision=lax.Precision.HIG...  10.2 us

profile of v1, /device:TPU:8, one launch (start us, length us, event | category | flops | bytes accessed | tf_op | source)
XLA Modules:
  0.0 343.2 jit_solution(8099907757003795867)
XLA Ops:
  0.6 0.5 broadcast.129
  1.2 1.5 reduce.6
  2.8 1.7 select_reduce_fusion
  4.6 0.9 concatenate.9
  5.5 0.7 convert_element_type.26
  6.3 1.0 fusion.3
  7.3 0.2 copy.78
  7.6 0.3 copy.79
  8.0 0.3 copy.80
  8.3 0.2 reshape.127
  8.5 21.4 %all_to_all.30 = f32[32,1,800]{2,1,0:T(1,128)S(1)} all-to-all(f32[32,1,800]{2,1,0:T(1,128)S(1)} %reshape.127), channel_id=1, replica_groups=mesh['table'=32,'scal'=8] {'table'}, dimensions={0} | all-to-all | bytes 204800 | tf_op jit(solution)/shard_map/all_to_all | solution.py:144
  29.9 0.6 broadcast.130
  30.5 1.0 reduce.7
  31.7 0.1 reshape.100
  31.8 14.7 %all_gather.3 = f32[5,40960]{1,0:T(8,128)S(1)} all-gather(f32[5,5120]{1,0:T(8,128)S(1)} %reshape.100), channel_id=1, replica_groups=mesh['table'=32,'scal'=8] {'scal'}, dimensions={1}, use_global_device_ids=true | all-gather | bytes 921600 | tf_op jit(solution)/shard_map/all_gather | solution.py:147
  46.5 0.2 compare_select_fusion
  46.7 2.4 slice_convert_fusion
  49.1 134.9 %gather_fusion = f32[40960,128]{1,0:T(8,128)} fusion(f32[4096,128]{1,0:T(8,128)S(1)} %copy-done, s32[40960]{0:T(1024)S(1)} %broadcast_clamp_fusion), kind=kCustom, calls=%fused_computation | custom fusion | bytes 42106880 | tf_op jit(solution)/shard_map/jit(_take)/gather | solution.py:149
  184.1 21.2 %copy.82 = f32[40960,128]{0,1:T(8,128)} copy(f32[40960,128]{1,0:T(8,128)} %gather_fusion) | data formatting | bytes 41943040 | tf_op jit(solution)/shard_map/jit(_take)/gather | solution.py:149
  205.3 0.3 pad_maximum_fusion.3
  205.6 0.6 pad_maximum_fusion.1
  206.2 0.3 broadcast_multiply_fusion.2
  206.5 0.5 broadcast_multiply_fusion.1
  207.0 0.6 pad_maximum_fusion
  207.6 3.4 broadcast_multiply_fusion
  211.0 6.1 %mul.131 = f32[32,40960]{1,0:T(8,128)} reshape(f32[2,2,2,4,40960]{4,3,2,1,0:T(4,128)} %broadcast_multiply_fusion) | data formatting | bytes 10485760 | tf_op jit(solution)/shard_map/mul | solution.py:41
  217.2 10.2 %multiply_reduce_fusion = f32[40960,4]{0,1:T(4,128)S(1)} fusion(f32[40960,4,32]{0,2,1:T(8,128)} %bitcast.85, f32[40960,32]{0,1:T(8,128)} %bitcast.86, pred[40960]{0:T(1024)(128)(4,1)S(1)} %compare_and_fusion), kind=kLoop, calls=%fused_computation.1 | loop fusion | flops 15564800 | bytes 26910720 | tf_op jit(solution)/shard_map/nsk,kn->sn/dot_general | solution.py:151
  227.4 0.4 copy.98
  228.5 14.6 %all_to_all.31 = f32[8,4,1,5120]{3,2,1,0:T(1,128)S(1)} all-to-all(f32[8,4,1,5120]{3,2,1,0:T(1,128)S(1)} %fusion.13), channel_id=1, replica_groups=mesh['table'=32,'scal'=8] {'scal'}, dimensions={0} | all-to-all | bytes 1310720 | tf_op jit(solution)/shard_map/all_to_all | solution.py:19
  243.1 1.8 reduce.2
  244.9 17.7 %reshape_reshape.3 = f32[32,32,32,5]{3,2,1,0:T(8,128)} reshape(f32[8,4,5120]{2,1,0:T(4,128)S(1)} %reduce.2) | data formatting | bytes 1310720 | tf_op jit(solution)/shard_map/reshape;reshape | solution.py:153
  262.6 12.5 %copy.83 = f32[32,32,32,5]{2,0,3,1:T(8,128)} copy(f32[32,32,32,5]{3,2,1,0:T(8,128)} %reshape_reshape.3) | data formatting | bytes 1310720 | tf_op jit(solution)/shard_map/reshape;reshape | solution.py:153
  275.1 2.7 reshape.129
  277.8 23.3 %all_to_all.32 = f32[32,1,5120]{2,1,0:T(1,128)S(1)} all-to-all(f32[32,1,5120]{2,1,0:T(1,128)S(1)} %reshape.129), channel_id=1, replica_groups=mesh['table'=32,'scal'=8] {'table'}, dimensions={0} | all-to-all | bytes 1310720 | tf_op jit(solution)/shard_map/all_to_all | solution.py:155
  301.2 2.2 reduce.8
  303.4 2.4 reshape.130
  305.8 3.0 copy.84
  308.8 1.5 fusion.2
  310.3 0.4 copy.94
  310.8 0.5 reshape.131
  311.2 17.0 %all_to_all.33 = f32[32,1,2048]{2,1,0:T(1,128)S(1)} all-to-all(f32[32,1,2048]{2,1,0:T(1,128)S(1)} %reshape.131), channel_id=1, replica_groups=mesh['table'=32,'scal'=8] {'table'}, dimensions={0} | all-to-all | bytes 524288 | tf_op jit(solution)/shard_map/all_to_all | solution.py:160
  328.2 1.3 reduce.9
  329.5 1.3 reshape.132
  330.9 1.4 bitcast_bitcast_fusion
  332.3 4.3 %copy.87 = f32[32,1,8,32,8]{4,3,2,0,1:T(8,128)} copy(f32[32,1,8,32,8]{0,4,2,3,1:T(8,128)S(1)} %bitcast_bitcast_fusion) | data formatting | bytes 524288 | tf_op jit(solution)/shard_map/all_to_all | solution.py:160
  336.7 4.0 %reshape.104 = f32[256,256]{1,0:T(8,128)S(1)} reshape(f32[32,1,8,32,8]{4,3,2,0,1:T(8,128)} %copy.87) | data formatting | bytes 524288 | tf_op jit(solution)/shard_map/reshape | solution.py:160
  340.7 1.3 fusion.22
  342.1 1.1 convolution_bitcast_fusion
  (37 shorter events, 1.5 us)
Async XLA Ops:
  0.6 48.5 %copy-start = (f32[4096,128]{1,0:T(8,128)S(1)}, f32[4096,128]{1,0:T(8,128)}, u32[]{:S(2)}) copy-start(f32[4096,128]{1,0:T(8,128)} %param.7) | copy-start | bytes 6291460
  184.1 21.2 %copy-start.4 = (f32[1,40960]{1,0:T(1,128)S(1)}, f32[1,40960]{1,0:T(1,128)}, u32[]{:S(2)}) copy-start(f32[1,40960]{1,0:T(1,128)} %get-tuple-element.5) | copy-start | bytes 491524
  184.1 21.2 %copy-start.5 = (f32[1,40960]{1,0:T(1,128)S(1)}, f32[1,40960]{1,0:T(1,128)}, u32[]{:S(2)}) copy-start(f32[1,40960]{1,0:T(1,128)} %get-tuple-element.10) | copy-start | bytes 491524
  184.1 21.5 %copy-start.3 = (f32[1,40960]{1,0:T(1,128)S(1)}, f32[1,40960]{1,0:T(1,128)}, u32[]{:S(2)}) copy-start(f32[1,40960]{1,0:T(1,128)} %get-tuple-element.12) | copy-start | bytes 491524
  211.0 6.1 %copy-start.6 = (s32[1,40960]{1,0:T(1,128)S(1)}, s32[1,40960]{1,0:T(1,128)}, u32[]{:S(2)}) copy-start(s32[1,40960]{1,0:T(1,128)} %get-tuple-element.2) | copy-start | bytes 491524
  330.9 12.3 %copy-start.1 = (f32[4096,128]{1,0:T(8,128)S(1)}, f32[4096,128]{1,0:T(8,128)}, u32[]{:S(2)}) copy-start(f32[4096,128]{1,0:T(8,128)} %param.7) | copy-start | bytes 6291460
  332.3 9.7 %copy-start.7 = (f32[256,256]{1,0:T(8,128)S(1)}, f32[256,256]{1,0:T(8,128)}, u32[]{:S(2)}) copy-start(f32[256,256]{1,0:T(8,128)} %constant.46.clone) | copy-start | bytes 786436
  342.1 1.1 copy-start.2
